TPU v7x, 32 devices: a whole 2x2x4 slice. The times are simulated.
32 devices in a mesh: expert: 8 (over y, x, core), dp: 4 (over z).
Axes of the slice: x: 2, y: 2, z: 4, core: 2. Of those that a mesh axis runs over, the one named last changes fastest.
Arguments:
- trunk: bfloat16 [768, 4096], P(('dp', 'expert')), may hold values from -6 to 6
- w_first: bfloat16 [8, 4096, 2048], P('expert'), may hold values from -0.09375 to 0.09375
- w_second: bfloat16 [8, 2048, 1024], P('expert'), may hold values from -0.125 to 0.125
- gates: bfloat16 [8, 8, 768], P('expert', None, 'dp'), may hold values from 0.049804688 to 1
- d_mixed: bfloat16 [768, 8, 1024], P(('dp', 'expert')), may hold values from -6 to 6
Outputs:
- mixed: bfloat16 [768, 8, 1024], P(('dp', 'expert'))
- d_trunk: bfloat16 [768, 4096], P(('dp', 'expert'))
- d_gates: bfloat16 [8, 8, 768], P('expert', None, 'dp')
- d_w_first: bfloat16 [8, 4096, 2048], P('expert', 'dp')
- d_w_second: bfloat16 [8, 2048, 1024], P('expert', 'dp')
All inputs are finite; a program needn't handle non-finite values.
Results may differ from a plain program's by a relative error of at most 0.015.
Values may be sent and summed in bfloat16 or wider, within the bound.
A program may use at most 128 MiB of HBM per device.

v0:
```python
import jax
import jax.numpy as jnp
from jax import lax
from jax.sharding import PartitionSpec as P


def on_device(trunk, w_first, w_second, gates, d_mixed):
    rows_all = lax.all_gather(trunk, "expert", axis=0, tiled=True)
    first = w_first[0]
    second = w_second[0]
    gate_here = gates[0]
    pre = jnp.dot(rows_all, first, preferred_element_type=jnp.float32)
    hidden = jax.nn.silu(pre).astype(jnp.bfloat16)
    output = jnp.dot(hidden, second, preferred_element_type=jnp.float32).astype(jnp.bfloat16)
    outs_each, gates_each = (
        lax.all_to_all(output[None], "expert", split_axis=1, concat_axis=0, tiled=True),
        lax.all_to_all(gate_here.T[None], "expert", split_axis=1, concat_axis=0, tiled=True),
    )
    mixed = jnp.einsum(
        "ert,ero->rto", gates_each, outs_each, preferred_element_type=jnp.float32
    ).astype(jnp.bfloat16)
    d_out_each = jnp.einsum(
        "ert,rto->ero", gates_each, d_mixed, preferred_element_type=jnp.float32
    ).astype(jnp.bfloat16)
    d_gate_each = jnp.einsum(
        "rto,ero->ert", d_mixed, outs_each, preferred_element_type=jnp.float32
    ).astype(jnp.bfloat16)
    back_out, back_gate = (
        lax.all_to_all(d_out_each, "expert", split_axis=0, concat_axis=1, tiled=True),
        lax.all_to_all(d_gate_each, "expert", split_axis=0, concat_axis=1, tiled=True),
    )
    d_output = back_out[0]
    d_gate = back_gate[0].T[None]
    d_hidden = lax.dot_general(
        d_output, second, (((1,), (1,)), ((), ())), preferred_element_type=jnp.float32
    )
    sig = jax.nn.sigmoid(pre)
    d_pre = (d_hidden * sig * (1.0 + pre * (1.0 - sig))).astype(jnp.bfloat16)
    piece = d_pre
    d_trunk = lax.psum_scatter(
        lax.dot_general(
            piece, first, (((1,), (1,)), ((), ())), preferred_element_type=jnp.float32
        ).astype(jnp.bfloat16),
        "expert",
        scatter_dimension=0,
        tiled=True,
    )
    piece = rows_all
    d_first = lax.psum_scatter(
        lax.dot_general(
            piece, d_pre, (((0,), (0,)), ((), ())), preferred_element_type=jnp.float32
        ).astype(jnp.bfloat16),
        "dp",
        scatter_dimension=0,
        tiled=True,
    )
    piece = hidden
    d_second = lax.psum_scatter(
        lax.dot_general(
            piece, d_output, (((0,), (0,)), ((), ())), preferred_element_type=jnp.float32
        ).astype(jnp.bfloat16),
        "dp",
        scatter_dimension=0,
        tiled=True,
    )
    return (mixed, d_trunk, d_gate, d_first[None], d_second[None])


def solution(mesh):
    in_specs = (
        P(("dp", "expert"), None),
        P("expert", None, None),
        P("expert", None, None),
        P("expert", None, "dp"),
        P(("dp", "expert"), None, None),
    )
    out_specs = (
        P(("dp", "expert"), None, None),
        P(("dp", "expert"), None),
        P("expert", None, "dp"),
        P("expert", "dp", None),
        P("expert", "dp", None),
    )
    return jax.shard_map(
        on_device, mesh=mesh, in_specs=in_specs, out_specs=out_specs, check_vma=False
    )
```

profile of v0, /device:TPU:0, one launch (start us, length us, event | category | flops | bytes accessed | tf_op | source)
XLA Modules:
  0.0 471.3 jit_solution(6701005433292984852)
XLA Ops:
  7.2 0.7 all-gather.2.cloned.1.call-update
  7.9 0.8 copy.31
  8.7 10.2 %all_to_all.42 = bf16[1,192,8]{2,0,1:T(2,128)(2,1)S(1)} all-to-all(bf16[1,192,8]{2,0,1:T(2,128)(2,1)S(1)} %copy.31), channel_id=1, replica_groups=mesh['expert'=8,'dp'=4] {'expert'}, dimensions={1} | all-to-all | bytes 6144 | tf_op jit(solution)/shard_map/all_to_all | solution.py:17
  19.5 1.0 copy.36
  20.5 3.5 all-to-all-start.2
  24.0 14.2 %all-gather.2.cloned.1.call-done = bf16[192,4096]{1,0:T(8,128)(2,1)} async-done(((bf16[24,4096]{1,0:T(8,128)(2,1)}), bf16[192,4096]{1,0:T(8,128)(2,1)}) %all-gather.2.cloned.1.call-update) | async-done | bytes 1572880 | tf_op jit(solution)/shard_map/all_gather | solution.py:8
  38.2 10.8 %fusion.2 = f32[192,2048]{1,0:T(8,128)} fusion(bf16[192,4096]{1,0:T(8,128)(2,1)} %all-gather.2.cloned.1.call-done, bf16[1,4096,2048]{2,1,0:T(8,128)(2,1)} %param.6), kind=kOutput, calls=%fused_computation.2 | convolution fusion | flops 3221225472 | bytes 19922944 | tf_op jit(solution)/shard_map/dot_general | solution.py:12
  49.0 4.5 fusion.17
  53.6 8.1 %convert_bitcast_fusion = bf16[4096,2048]{0,1:T(8,128)(2,1)} fusion(bf16[192,2048]{1,0:T(8,128)(2,1)S(1)} %fusion.17, bf16[192,4096]{1,0:T(8,128)(2,1)S(1)} %copy-done.1), kind=kOutput, calls=%fused_computation.4 | convolution fusion | flops 3229614080 | bytes 19136512 | tf_op jit(solution)/shard_map/dot_general | solution.py:50
  61.8 12.6 %fusion.4 = bf16[192,4096]{1,0:T(8,128)(2,1)} fusion(bf16[192,2048]{1,0:T(8,128)(2,1)S(1)} %fusion.17, bf16[1,4096,2048]{2,1,0:T(8,128)(2,1)} %param.6), kind=kOutput, calls=%fused_computation.5 | convolution fusion | flops 3222011904 | bytes 19136512 | tf_op jit(solution)/shard_map/dot_general | solution.py:41
  74.6 1.2 copy-done.2
  75.8 3.3 convolution_convert_fusion
  79.1 3.2 fusion.25
  83.5 2.9 reduce
  86.7 10.8 %all_to_all.43 = bf16[8,2,12288]{2,1,0:T(2,128)(2,1)S(1)} all-to-all(bf16[8,2,12288]{2,1,0:T(2,128)(2,1)S(1)} %reshape.24), channel_id=1, replica_groups=mesh['expert'=8,'dp'=4] {'expert'}, dimensions={0} | all-to-all | bytes 786432 | tf_op jit(solution)/shard_map/all_to_all | solution.py:16
  98.4 0.7 copy.38
  99.1 3.3 all-to-all-start.3
  102.5 1.1 fusion.23
  103.6 3.6 all-to-all-done.3
  107.1 0.7 squeeze.19
  107.8 234.5 %reduce-scatter.6.cloned.1.call-done = bf16[1024,2048]{0,1:T(8,128)(2,1)} async-done(((bf16[4096,2048]{0,1:T(8,128)(2,1)}), bf16[1024,2048]{0,1:T(8,128)(2,1)}) %reduce-scatter.6.cloned.1.call-update) | async-done | bytes 4194320 | tf_op jit(solution)/shard_map/reduce_scatter | solution.py:49
  342.3 6.4 %copy.40 = bf16[1,1024,2048]{2,1,0:T(8,128)(2,1)} copy(bf16[1,1024,2048]{1,2,0:T(8,128)(2,1)} %bitcast.62) | data formatting | bytes 8388608
  348.7 36.4 %reduce-scatter.4.cloned.1.call-done = bf16[24,4096]{1,0:T(8,128)(2,1)} async-done(((bf16[192,4096]{1,0:T(8,128)(2,1)}), bf16[24,4096]{1,0:T(8,128)(2,1)}) %reduce-scatter.4.cloned.1.call-update) | async-done | bytes 196624 | tf_op jit(solution)/shard_map/reduce_scatter | solution.py:40
  385.2 79.6 %reduce-scatter.8.cloned.1.call-done = bf16[512,1024]{1,0:T(8,128)(2,1)} async-done(((bf16[2048,1024]{1,0:T(8,128)(2,1)}), bf16[512,1024]{1,0:T(8,128)(2,1)}) %reduce-scatter.8.cloned.1.call-update) | async-done | bytes 1048592 | tf_op jit(solution)/shard_map/reduce_scatter | solution.py:58
  (24 shorter events, 3.2 us)
Async XLA Ops:
  7.2 12.1 %copy-start = (bf16[24,8,1024]{2,1,0:T(8,128)(2,1)S(1)}, bf16[24,8,1024]{2,1,0:T(8,128)(2,1)}, u32[]{:S(2)}) copy-start(bf16[24,8,1024]{2,1,0:T(8,128)(2,1)} %param.9) | copy-start | bytes 1179652
  7.2 31.0 %all-gather.2.cloned.1.call-start = ((), (), s32[]{:S(2)}) async-start(), calls=%async_computation.7 | async-start | bytes 1769472 | tf_op jit(solution)/shard_map/all_gather | solution.py:8
  20.5 28.6 %all-to-all-start.2 = ((bf16[8,24,1024]{2,1,0:T(8,128)(2,1)}), bf16[8,24,1024]{2,1,0:T(8,128)(2,1)S(1)}, u32[]{:S(2)}, u32[]{:S(2)}) async-start(bf16[8,24,1024]{2,1,0:T(8,128)(2,1)} %copy.36), calls=%async_computation.2 | async-start | bytes 786432 | tf_op jit(solution)/shard_map/all_to_all | solution.py:29
  23.9 318.4 %reduce-scatter.6.cloned.1.call-start = ((), (), s32[]{:S(2)}) async-start(), calls=%async_computation.9 | async-start | bytes 20971520 | tf_op jit(solution)/shard_map/reduce_scatter | solution.py:49
  49.0 4.5 copy-start.1
  61.7 323.5 %reduce-scatter.4.cloned.1.call-start = ((), (), s32[]{:S(2)}) async-start(), calls=%async_computation.8 | async-start | bytes 1769472 | tf_op jit(solution)/shard_map/reduce_scatter | solution.py:40
  74.4 1.4 copy-start.2
  74.4 390.3 %reduce-scatter.8.cloned.1.call-start = ((), (), s32[]{:S(2)}) async-start(), calls=%async_computation.10 | async-start | bytes 5242880 | tf_op jit(solution)/shard_map/reduce_scatter | solution.py:58
  99.1 8.0 %all-to-all-start.3 = ((bf16[8,24,8]{1,2,0:T(8,128)(2,1)}), bf16[8,24,8]{1,2,0:T(8,128)(2,1)S(1)}, u32[]{:S(2)}, u32[]{:S(2)}) async-start(bf16[8,24,8]{1,2,0:T(8,128)(2,1)} %copy.38), calls=%async_computation.4 | async-start | bytes 32768 | tf_op jit(solution)/shard_map/all_to_all | solution.py:30
Sparse Core Ops, SparseCore 0:
  9.9 28.2 all-gather.1
  61.8 280.4 reduce-scatter.5
  346.2 38.9 reduce-scatter.3
  387.9 76.7 reduce-scatter.7
where the time goes:
time: 472 us; the launch traced here: 471 us
  waiting for transfers between devices  369 us (78%)
  matrix products  44.3 us (9%)
  blocking collectives  21 us (4%)
  between operations  13.9 us (3%)
  local copies, waits for them, and re-layouts  12.9 us (3%)
  starting transfers between devices  7.13 us (2%)
    reduce_scatter x1, waiting for transfers between devices, on_device(): lax.psum_scatter(lax.dot_general(piece, d_pre, (((0,), (0,)), ((), ())),...  234 us
    reduce_scatter x1, waiting for transfers between devices, on_device(): lax.psum_scatter(lax.dot_general(piece, d_output, (((0,), (0,)), ((), ())...  79.6 us
    reduce_scatter x1, waiting for transfers between devices, on_device(): lax.psum_scatter(lax.dot_general(piece, first, (((1,), (1,)), ((), ())),...  36.4 us
    all_gather x1, waiting for transfers between devices, on_device(): rows_all = lax.all_gather(trunk, 'expert', axis=0, tiled=True)  14.2 us
    dot_general x1, matrix products, on_device(): lax.dot_general(piece, first, (((1,), (1,)), ((), ())), preferred_element...  12.6 us
    all_to_all x1, blocking collectives, on_device(): lax.all_to_all(output[None], 'expert', split_axis=1, concat_axis=0, tiled...  10.8 us
    dot_general x1, matrix products, on_device(): pre = jnp.dot(rows_all, first, preferred_element_type=jnp.float32)  10.8 us
    all_to_all x1, blocking collectives, on_device(): lax.all_to_all(gate_here.T[None], 'expert', split_axis=1, concat_axis=0,...  10.2 us
  transfers between devices with their start and end apart: 6, of which 5 were waited for; matrix products, arithmetic and copies ran while one was open for 10% of the time, Pallas kernels for 0%

commit v1 on v0

--- a/solution.py
+++ b/solution.py
@@ -14,7 +14,15 @@
     output = jnp.dot(hidden, second, preferred_element_type=jnp.float32).astype(jnp.bfloat16)
     outs_each, gates_each = (
         lax.all_to_all(output[None], "expert", split_axis=1, concat_axis=0, tiled=True),
-        lax.all_to_all(gate_here.T[None], "expert", split_axis=1, concat_axis=0, tiled=True),
+        jnp.concatenate(
+            lax.all_to_all(
+                jnp.stack(jnp.split(gate_here.T[None], lax.axis_size("expert"), axis=1)),
+                "expert",
+                0,
+                0,
+            ),
+            axis=0,
+        ),
     )
     mixed = jnp.einsum(
         "ert,ero->rto", gates_each, outs_each, preferred_element_type=jnp.float32

time: 472 us -> 476 us (level)
  blocking collectives: 21 us -> 9.82 us
  waiting for transfers between devices: 369 us -> 375 us
  local copies, waits for them, and re-layouts: 12.9 us -> 18.8 us
    all_to_all x2 -> x1, blocking collectives: 21 us -> 9.82 us  [on_device(): lax.all_to_all(jnp.stack(jnp.split(gate_here.T[None], lax.axis_size('expe...]
    all_to_all x0 -> x1, waiting for transfers between devices: none -> 8.13 us  [on_device(): lax.all_to_all(output[None], 'expert', split_axis=1, concat_axis=0, tiled...]
    unnamed x11 -> x18, local copies, waits for them, and re-layouts: 8.85 us -> 14.8 us
  transfers between devices with their start and end apart: 6 -> 7, of which waited for: 5 -> 6; matrix products, arithmetic and copies ran while one was open for 10% -> 11% of each run, Pallas kernels for 0% -> 0%
where the time goes in v1:
time: 476 us; the launch traced here: 475 us
  waiting for transfers between devices  375 us (79%)
  matrix products  44.3 us (9%)
  local copies, waits for them, and re-layouts  18.8 us (4%)
  between operations  13.9 us (3%)
  starting transfers between devices  10.6 us (2%)
  blocking collectives  9.82 us (2%)
    reduce_scatter x1, waiting for transfers between devices, on_device(): lax.psum_scatter(lax.dot_general(piece, d_pre, (((0,), (0,)), ((), ())),...  233 us
    reduce_scatter x1, waiting for transfers between devices, on_device(): lax.psum_scatter(lax.dot_general(piece, d_output, (((0,), (0,)), ((), ())...  79.6 us
    reduce_scatter x1, waiting for transfers between devices, on_device(): lax.psum_scatter(lax.dot_general(piece, first, (((1,), (1,)), ((), ())),...  36.4 us
    unnamed x18, local copies, waits for them, and re-layouts  14.8 us
    all_gather x1, waiting for transfers between devices, on_device(): rows_all = lax.all_gather(trunk, 'expert', axis=0, tiled=True)  13 us
    dot_general x1, matrix products, on_device(): lax.dot_general(piece, first, (((1,), (1,)), ((), ())), preferred_element...  12.6 us
    dot_general x1, matrix products, on_device(): pre = jnp.dot(rows_all, first, preferred_element_type=jnp.float32)  10.8 us
    all_to_all x1, blocking collectives, on_device(): lax.all_to_all(jnp.stack(jnp.split(gate_here.T[None], lax.axis_size('expe...  9.82 us
  transfers between devices with their start and end apart: 7, of which 6 were waited for; matrix products, arithmetic and copies ran while one was open for 11% of the time, Pallas kernels for 0%

profile of v1, /device:TPU:0, one launch (start us, length us, event | category | flops | bytes accessed | tf_op | source)
XLA Modules:
  0.0 474.9 jit_solution(7292121149071244583)
XLA Ops:
  8.6 0.8 constant_dynamic-update-slice_fusion.6
  11.6 0.8 constant_dynamic-update-slice_fusion.2
  13.9 9.8 %all_to_all.35 = bf16[8,1,24,8]{2,3,1,0:T(8,128)(2,1)S(1)} all-to-all(bf16[8,1,24,8]{2,3,1,0:T(8,128)(2,1)S(1)} %constant_dynamic-update-slice_fusion), channel_id=1, replica_groups=mesh['expert'=8,'dp'=4] {'expert'}, dimensions={0} | all-to-all | bytes 6144 | tf_op jit(solution)/shard_map/all_to_all | solution.py:18
  24.2 1.0 copy.173
  25.1 3.5 all-to-all-start.2
  28.7 13.0 %all-gather.2.cloned.1.call-done = bf16[192,4096]{1,0:T(8,128)(2,1)} async-done(((bf16[24,4096]{1,0:T(8,128)(2,1)}), bf16[192,4096]{1,0:T(8,128)(2,1)}) %all-gather.2.cloned.1.call-update) | async-done | bytes 1572880 | tf_op jit(solution)/shard_map/all_gather | solution.py:8
  41.6 10.8 %fusion.2 = f32[192,2048]{1,0:T(8,128)} fusion(bf16[192,4096]{1,0:T(8,128)(2,1)} %all-gather.2.cloned.1.call-done, bf16[1,4096,2048]{2,1,0:T(8,128)(2,1)} %param.6), kind=kOutput, calls=%fused_computation.2 | convolution fusion | flops 3221225472 | bytes 19922944 | tf_op jit(solution)/shard_map/dot_general | solution.py:12
  52.4 4.5 fusion.17
  57.0 8.1 %convert_bitcast_fusion = bf16[4096,2048]{0,1:T(8,128)(2,1)} fusion(bf16[192,2048]{1,0:T(8,128)(2,1)S(1)} %fusion.17, bf16[192,4096]{1,0:T(8,128)(2,1)S(1)} %copy-done.1), kind=kOutput, calls=%fused_computation.4 | convolution fusion | flops 3229614080 | bytes 19136512 | tf_op jit(solution)/shard_map/dot_general | solution.py:58
  65.2 12.6 %fusion.4 = bf16[192,4096]{1,0:T(8,128)(2,1)} fusion(bf16[192,2048]{1,0:T(8,128)(2,1)S(1)} %fusion.17, bf16[1,4096,2048]{2,1,0:T(8,128)(2,1)} %param.6), kind=kOutput, calls=%fused_computation.5 | convolution fusion | flops 3222011904 | bytes 19136512 | tf_op jit(solution)/shard_map/dot_general | solution.py:49
  78.0 1.2 copy-done.2
  79.2 3.3 convolution_convert_fusion
  82.5 3.2 fusion.24
  86.9 2.9 reduce
  89.8 1.0 reshape.25
  90.8 3.5 all-to-all-start.1
  94.4 8.1 %all-to-all-done.1 = bf16[8,2,12288]{2,1,0:T(2,128)(2,1)S(1)} async-done(((bf16[8,2,12288]{2,1,0:T(2,128)(2,1)}), bf16[8,2,12288]{2,1,0:T(2,128)(2,1)S(1)}, u32[]{:S(2)}, u32[]{:S(2)}) %all-to-all-start.1) | async-done | bytes 393248 | tf_op jit(solution)/shard_map/all_to_all | solution.py:16
  104.1 3.3 all-to-all-start.3
  107.4 1.1 convolution_convert_fusion.2
  108.5 3.6 all-to-all-done.3
  112.8 233.2 %reduce-scatter.6.cloned.1.call-done = bf16[1024,2048]{0,1:T(8,128)(2,1)} async-done(((bf16[4096,2048]{0,1:T(8,128)(2,1)}), bf16[1024,2048]{0,1:T(8,128)(2,1)}) %reduce-scatter.6.cloned.1.call-update) | async-done | bytes 4194320 | tf_op jit(solution)/shard_map/reduce_scatter | solution.py:57
  346.0 6.4 %copy.177 = bf16[1,1024,2048]{2,1,0:T(8,128)(2,1)} copy(bf16[1,1024,2048]{1,2,0:T(8,128)(2,1)} %bitcast.93) | data formatting | bytes 8388608
  352.4 36.4 %reduce-scatter.4.cloned.1.call-done = bf16[24,4096]{1,0:T(8,128)(2,1)} async-done(((bf16[192,4096]{1,0:T(8,128)(2,1)}), bf16[24,4096]{1,0:T(8,128)(2,1)}) %reduce-scatter.4.cloned.1.call-update) | async-done | bytes 196624 | tf_op jit(solution)/shard_map/reduce_scatter | solution.py:48
  388.8 79.6 %reduce-scatter.8.cloned.1.call-done = bf16[512,1024]{1,0:T(8,128)(2,1)} async-done(((bf16[2048,1024]{1,0:T(8,128)(2,1)}), bf16[512,1024]{1,0:T(8,128)(2,1)}) %reduce-scatter.8.cloned.1.call-update) | async-done | bytes 1048592 | tf_op jit(solution)/shard_map/reduce_scatter | solution.py:66
  (31 shorter events, 9.5 us)
Async XLA Ops:
  7.2 16.7 %copy-start = (bf16[24,8,1024]{2,1,0:T(8,128)(2,1)S(1)}, bf16[24,8,1024]{2,1,0:T(8,128)(2,1)}, u32[]{:S(2)}) copy-start(bf16[24,8,1024]{2,1,0:T(8,128)(2,1)} %param.9) | copy-start | bytes 1179652
  7.2 34.4 %all-gather.2.cloned.1.call-start = ((), (), s32[]{:S(2)}) async-start(), calls=%async_computation.7 | async-start | bytes 1769472 | tf_op jit(solution)/shard_map/all_gather | solution.py:8
  25.1 27.3 %all-to-all-start.2 = ((bf16[8,24,1024]{2,1,0:T(8,128)(2,1)}), bf16[8,24,1024]{2,1,0:T(8,128)(2,1)S(1)}, u32[]{:S(2)}, u32[]{:S(2)}) async-start(bf16[8,24,1024]{2,1,0:T(8,128)(2,1)} %copy.173), calls=%async_computation.2 | async-start | bytes 786432 | tf_op jit(solution)/shard_map/all_to_all | solution.py:37
  28.6 317.4 %reduce-scatter.6.cloned.1.call-start = ((), (), s32[]{:S(2)}) async-start(), calls=%async_computation.9 | async-start | bytes 20971520 | tf_op jit(solution)/shard_map/reduce_scatter | solution.py:57
  52.4 4.5 copy-start.1
  65.1 323.7 %reduce-scatter.4.cloned.1.call-start = ((), (), s32[]{:S(2)}) async-start(), calls=%async_computation.8 | async-start | bytes 1769472 | tf_op jit(solution)/shard_map/reduce_scatter | solution.py:48
  77.8 1.4 copy-start.2
  77.8 390.6 %reduce-scatter.8.cloned.1.call-start = ((), (), s32[]{:S(2)}) async-start(), calls=%async_computation.10 | async-start | bytes 5242880 | tf_op jit(solution)/shard_map/reduce_scatter | solution.py:66
  90.8 11.7 %all-to-all-start.1 = ((bf16[8,2,12288]{2,1,0:T(2,128)(2,1)}), bf16[8,2,12288]{2,1,0:T(2,128)(2,1)S(1)}, u32[]{:S(2)}, u32[]{:S(2)}) async-start(bf16[8,2,12288]{2,1,0:T(2,128)(2,1)} %reshape.25), calls=%async_computation.1 | async-start | bytes 786432 | tf_op jit(solution)/shard_map/all_to_all | solution.py:16
  104.1 8.0 %all-to-all-start.3 = ((bf16[8,24,8]{1,2,0:T(8,128)(2,1)}), bf16[8,24,8]{1,2,0:T(8,128)(2,1)S(1)}, u32[]{:S(2)}, u32[]{:S(2)}) async-start(bf16[8,24,8]{1,2,0:T(8,128)(2,1)} %copy.175), calls=%async_computation.4 | async-start | bytes 32768 | tf_op jit(solution)/shard_map/all_to_all | solution.py:38
Sparse Core Ops, SparseCore 0:
  9.9 31.7 all-gather.1
  65.2 280.7 reduce-scatter.5
  349.9 38.9 reduce-scatter.3
  391.5 76.7 reduce-scatter.7
